TPU v7x, 32 devices: a whole 2x2x4 slice. The times are simulated.
32 devices in a mesh: bead: 8 (over y, x, core), space: 4 (over z).
Axes of the slice: x: 2, y: 2, z: 4, core: 2. Of those that a mesh axis runs over, the one named last changes fastest.
Arguments:
- positions: float32 [32, 3, 2048], P('bead', None, 'space'), may hold values from -3 to 3
- momenta: float32 [32, 3, 2048], P('bead', None, 'space'), may hold values from -6 to 6
- neighbours: int32 [32, 2048], P(None, 'space'), may hold values from 0 to 767, as said below
- ghost_rows: int32 [1024], P('space'), may hold values from 0 to 511
- species: int32 [2048], P('space'), may hold values from 0 to 1
- species_scale: float32 [2], replicated, may hold values from 0.5 to 2
- mass_table: float32 [2], replicated, may hold values from 0.25 to 1
- w_in: float32 [128, 8], replicated, may hold values from -2 to 2
- w_out: float32 [8, 128], replicated, may hold values from -0.5 to 0.5
Outputs:
- new_positions: float32 [32, 3, 2048], P('bead', None, 'space')
- new_momenta: float32 [32, 3, 2048], P('bead', None, 'space')
Inputs may be any that keep to these rules, and one draw needn't show every extreme that they name: `neighbours`: A neighbour entry indexes the window of its atom's domain; slots beyond an atom's live count hold the atom's own position 128 + (atom index mod 512); every atom has at least 8 live slots. `ghost_rows`: domain d's block is entries 2 * 128 * d to 2 * 128 * (d + 1) - 1; entries index atoms within domain d.
All inputs are finite; a program needn't handle non-finite values.
Results may differ from a plain program's by a relative error of at most 0.0003.
Values sent between devices are 32-bit elements; how exact they have to be, the bound alone decides.
A program may use at most 64 MiB of HBM per device.

v0:
```python
import jax
import jax.numpy as jnp
import numpy as np
from jax import lax
from jax.sharding import PartitionSpec as P

BEADS = 32
CB = 4
NINNER = 3


polymer_freq = 10.0
outer_step = 6.0
pair_width = 1.0
pair_strength = 1.0
highest = lax.Precision.HIGHEST


def with_halo(block, sides, width):
    for axis, dim in sides:
        count = lax.axis_size(axis)
        forward = [(i, i + 1) for i in range(count - 1)]
        forward.append((count - 1, 0))
        backward = [(target, source) for source, target in forward]
        low = lax.ppermute(
            lax.slice_in_dim(block, block.shape[dim] - width, None, axis=dim), axis, forward
        )
        high = lax.ppermute(lax.slice_in_dim(block, 0, width, axis=dim), axis, backward)
        block = jnp.concatenate([low, block, high], axis=dim)
    return block


def mode_matrix(count):
    beadpos = np.arange(count)[None, :]
    modeidx = np.arange(count)[:, None]
    middle = count // 2
    cosine = np.sqrt(2.0 / count) * np.cos(2.0 * np.pi * beadpos * modeidx / count)
    sine_rows = np.sqrt(2.0 / count) * np.sin(2.0 * np.pi * beadpos * modeidx / count)
    matrix = np.where(modeidx < middle, cosine, sine_rows)
    matrix = np.where(modeidx == 0, 1.0 / np.sqrt(count), matrix)
    matrix = np.where(modeidx == middle, np.cos(np.pi * beadpos) / np.sqrt(count), matrix)
    return matrix


def mode_scales(count, inner_step):
    frequency = 2.0 * polymer_freq * np.sin(np.pi * np.arange(count) / count)
    nonzero = np.where(frequency > 0, frequency, 1.0)
    cosine = np.cos(frequency * inner_step)
    drift_gain = np.where(frequency > 0, np.sin(frequency * inner_step) / nonzero, inner_step)
    spring = frequency * np.sin(frequency * inner_step)
    return (cosine, drift_gain, spring)


def polymer_tables(count, inner_step):
    modes = mode_matrix(count)
    cosine, drift_gain, spring = mode_scales(count, inner_step)
    persist = modes.T @ (cosine[:, None] * modes)
    coupling = modes.T @ (drift_gain[:, None] * modes)
    restoring = -(modes.T @ (spring[:, None] * modes))
    return (
        jnp.asarray(persist, jnp.float32),
        jnp.asarray(coupling, jnp.float32),
        jnp.asarray(restoring, jnp.float32),
    )


def contraction(count, fewer):
    full_modes = mode_matrix(count)
    small_modes = mode_matrix(fewer)
    kept = list(range(fewer // 2 + 1)) + list(range(count - fewer // 2 + 1, count))
    contract = np.sqrt(fewer / count) * (small_modes.T @ full_modes[kept])
    expand = count / fewer * contract.T
    return (jnp.asarray(contract, jnp.float32), jnp.asarray(expand, jnp.float32))


def radial_rates(count):
    return 0.2 * 2.0 ** (np.arange(count) / 2.0)


def species_lookup(species, table):
    kinds = jnp.arange(table.shape[0], dtype=jnp.int32)
    return jnp.sum(jnp.where(species[None, :] == kinds[:, None], table[:, None], 0.0), axis=0)


def pair_forces(extended, targets, centres):
    others = extended[:, targets]
    middle = extended[:, centres]
    offsets = others[:3] - middle[:3, None, :]
    squared = jnp.sum(offsets * offsets, axis=0)
    weights = others[3] * jnp.exp(-squared / pair_width)
    return pair_strength * middle[3] * jnp.sum(weights[None] * offsets, axis=1)


def learned_forces(extended, charges, targets, centres, w_in, w_out):
    live = (targets != centres[None, :]).astype(jnp.float32)
    weights = charges[targets] * live
    others = extended[:, targets]
    middle = extended[:, centres]
    offsets = others - middle[:, None, :]
    squared = jnp.sum(offsets * offsets, axis=0)
    rates = jnp.asarray(radial_rates(w_in.shape[1]), jnp.float32)
    basis = jnp.exp(-rates[:, None, None] * squared[None])
    message = jnp.sum(weights[None] * basis, axis=1) / targets.shape[0]
    hidden = jax.nn.silu(
        jnp.dot(w_in, message, precision=highest, preferred_element_type=jnp.float32)
    )
    radial = jnp.dot(w_out, hidden, precision=highest, preferred_element_type=jnp.float32)
    profile = jnp.sum(radial[:, None, :] * basis, axis=0)
    return jnp.sum((weights * profile)[None] * offsets, axis=1)


def body(
    positions, momenta, neighbours, ghost_rows, species, species_scale, mass_table, w_in, w_out
):
    per_device = positions.shape[0]
    atom_count = positions.shape[2]
    ghosts = ghost_rows.shape[0] // 2
    bead_devices = lax.axis_size("bead")
    device = lax.axis_index("bead")
    inner_step = outer_step / NINNER
    persist, coupling, restoring = polymer_tables(BEADS, inner_step)
    contract, expand = contraction(BEADS, CB)
    contract_mine = lax.dynamic_slice_in_dim(contract, device * per_device, per_device, 1)
    expand_mine = lax.dynamic_slice_in_dim(expand, device * per_device, per_device, 0)
    charges = species_lookup(species, species_scale)
    masses = species_lookup(species, mass_table)
    centres = ghosts + jnp.arange(atom_count, dtype=jnp.int32)
    charge_rows = jnp.broadcast_to(charges[None, None, :], (per_device, 1, atom_count))

    def cheap_forces(coords):
        stacked = jnp.concatenate([coords, charge_rows], axis=1)
        sends = stacked[:, :, ghost_rows]
        padded = with_halo(sends, (("space", 2),), ghosts)
        extended = jnp.concatenate(
            [padded[:, :, :ghosts], stacked, padded[:, :, 3 * ghosts :]], axis=2
        )
        forces = lax.map(lambda single: pair_forces(single, neighbours, centres), extended)
        return (forces, extended)

    def expensive_forces(bead_window, charge_window):
        window_term = jnp.einsum(
            "cb,bxa->cxa", contract_mine, bead_window[:, :3], precision=highest
        )
        extended = lax.psum(window_term, "bead")
        groups = bead_devices // CB
        share = atom_count // groups
        member = device // groups
        offset = device % groups * share
        chosen = lax.dynamic_index_in_dim(extended, member, 0, keepdims=False)
        targets = lax.dynamic_slice_in_dim(neighbours, offset, share, 1)
        middle = ghosts + offset + jnp.arange(share, dtype=jnp.int32)
        piece = learned_forces(chosen, charge_window, targets, middle, w_in, w_out)
        whole = lax.all_gather(piece, "bead", axis=1, tiled=True).reshape(3, CB, atom_count)
        result = jnp.einsum("bc,xca->bxa", expand_mine, whole, precision=highest)
        return result

    coords = positions
    cheap_now, bead_window = cheap_forces(coords)
    charge_window = bead_window[0, 3]
    moments = momenta + 0.5 * outer_step * expensive_forces(bead_window, charge_window)
    for repeat in range(NINNER):
        moments = moments + 0.5 * inner_step * cheap_now
        persist_mine = lax.dynamic_slice_in_dim(persist, device * per_device, per_device, 0)
        coupling_mine = lax.dynamic_slice_in_dim(coupling, device * per_device, per_device, 0)
        restoring_mine = lax.dynamic_slice_in_dim(restoring, device * per_device, per_device, 0)
        empty = jnp.zeros_like(coords)
        pieces = (
            lax.all_gather(coords, "bead", axis=0, tiled=True),
            lax.all_gather(moments, "bead", axis=0, tiled=True),
        )
        number = pieces[0].shape[0]
        block_persist = lax.slice_in_dim(persist_mine, 0, number, axis=1)
        block_coupling = lax.slice_in_dim(coupling_mine, 0, number, axis=1)
        block_restoring = lax.slice_in_dim(restoring_mine, 0, number, axis=1)
        new_coords = (
            empty
            + jnp.einsum("ab,bxn->axn", block_persist, pieces[0], precision=highest)
            + jnp.einsum("ab,bxn->axn", block_coupling, pieces[1], precision=highest) / masses
        )
        new_moments = (
            empty
            + jnp.einsum("ab,bxn->axn", block_persist, pieces[1], precision=highest)
            + jnp.einsum("ab,bxn->axn", block_restoring, pieces[0], precision=highest) * masses
        )
        coords = new_coords
        moments = new_moments
        cheap_now, bead_window = cheap_forces(coords)
        moments = moments + 0.5 * inner_step * cheap_now
    moments = moments + 0.5 * outer_step * expensive_forces(bead_window, charge_window)
    return (coords, moments)


def solution(mesh):
    in_specs = (
        P("bead", None, "space"),
        P("bead", None, "space"),
        P(None, "space"),
        P("space"),
        P("space"),
        P(),
        P(),
        P(),
        P(),
    )
    out_specs = (P("bead", None, "space"), P("bead", None, "space"))
    return jax.shard_map(body, mesh=mesh, in_specs=in_specs, out_specs=out_specs, check_vma=False)
```

profile of v0, /device:TPU:0, one launch (start us, length us, event | category | flops | bytes accessed | tf_op | source)
XLA Modules:
  0.0 1257.4 jit_solution(7958238049162234204)
XLA Ops:
  11.3 9.5 all_gather.24
  22.6 249.8 %while.44 = (s32[]{:T(128)}, f32[4,3,512]{2,0,1:T(4,128)S(1)}, f32[4,4,768]{2,0,1:T(4,128)S(1)}, s32[32,512]{1,0:T(8,128)}, s32[]{:T(128)}, /*index=5*/s32[]{:T(128)}) while((s32[]{:T(128)}, f32[4,3,512]{2,0,1:T(4,128)S(1)}, f32[4,4,768]{2,0,1:T(4,128)S(1)}, s32[32,512]{1,0:T(8,128)}, s32[]{:T(128)}, /*index=5*/s32[]{:T(128)}) %tuple.94), condition=%wide.region_9.10_spmd.clone, body=%wide.region_6.9_spmd.clone.sunk | while | flops 379906 | bytes 2381909 | solution.py:137
  25.1 54.4 %gather_fusion = f32[16384,4]{1,0:T(8,128)} fusion(f32[4,768]{0,1:T(8,128)S(1)} %bitcast.252, s32[16384]{0:T(1024)S(1)} %broadcast_clamp_fusion.9), kind=kCustom, calls=%fused_computation.1.clone.clone.1 | custom fusion | bytes 589824 | tf_op jit(solution)/shard_map/while/body/eval_jaxpr/gather | solution.py:86
  87.6 54.4 %gather_fusion = f32[16384,4]{1,0:T(8,128)} fusion(f32[4,768]{0,1:T(8,128)S(1)} %bitcast.252, s32[16384]{0:T(1024)S(1)} %broadcast_clamp_fusion.9), kind=kCustom, calls=%fused_computation.1.clone.clone.1 | custom fusion | bytes 589824 | tf_op jit(solution)/shard_map/while/body/eval_jaxpr/gather | solution.py:86
  150.0 54.4 %gather_fusion = f32[16384,4]{1,0:T(8,128)} fusion(f32[4,768]{0,1:T(8,128)S(1)} %bitcast.252, s32[16384]{0:T(1024)S(1)} %broadcast_clamp_fusion.9), kind=kCustom, calls=%fused_computation.1.clone.clone.1 | custom fusion | bytes 589824 | tf_op jit(solution)/shard_map/while/body/eval_jaxpr/gather | solution.py:86
  212.5 54.4 %gather_fusion = f32[16384,4]{1,0:T(8,128)} fusion(f32[4,768]{0,1:T(8,128)S(1)} %bitcast.252, s32[16384]{0:T(1024)S(1)} %broadcast_clamp_fusion.9), kind=kCustom, calls=%fused_computation.1.clone.clone.1 | custom fusion | bytes 589824 | tf_op jit(solution)/shard_map/while/body/eval_jaxpr/gather | solution.py:86
  272.6 23.9 %psum.14 = f32[4,3,768]{2,0,1:T(4,128)S(1)} all-reduce(f32[4,3,768]{2,0,1:T(4,128)S(1)} %fusion.68), channel_id=1, replica_groups=mesh['bead'=8,'space'=4] {'bead'}, use_global_device_ids=true, to_apply=%region_1.2 | all-reduce | flops 9216 | bytes 73728 | tf_op jit(solution)/shard_map/psum | solution.py:144
  296.6 32.9 %gather_fusion.9 = f32[8192]{0:T(1024)S(1)} fusion(f32[768]{0:T(1024)S(1)} %slice_reduce_fusion.4, s32[8192]{0:T(1024)S(1)} %broadcast_clamp_fusion.4), kind=kCustom, calls=%fused_computation.9 | custom fusion | bytes 98304 | tf_op jit(solution)/shard_map/gather | solution.py:96
  329.7 27.7 %gather_fusion.10 = f32[8192,3]{1,0:T(8,128)} fusion(f32[3,768]{0,1:T(8,128)S(1)} %bitcast.295, s32[8192]{0:T(1024)S(1)} %broadcast_clamp_fusion.4), kind=kCustom, calls=%fused_computation.10 | custom fusion | bytes 229376 | tf_op jit(solution)/shard_map/gather | solution.py:97
  364.1 11.1 all_gather.25
  376.4 8.5 all_gather.26
  386.2 9.1 all_gather.27
  402.5 246.4 %while.45 = (s32[]{:T(128)}, f32[4,3,512]{2,0,1:T(4,128)S(1)}, f32[4,4,768]{2,0,1:T(4,128)S(1)}, s32[32,512]{1,0:T(8,128)S(1)}, s32[]{:T(128)}, /*index=5*/s32[]{:T(128)}) while((s32[]{:T(128)}, f32[4,3,512]{2,0,1:T(4,128)S(1)}, f32[4,4,768]{2,0,1:T(4,128)S(1)}, s32[32,512]{1,0:T(8,128)S(1)}, s32[]{:T(128)}, ...), condition=%wide.region_14.15_spmd.clone, body=%wide.region_11.14_spmd.clone.sunk | while | flops 379906 | bytes 2381909 | solution.py:137
  404.2 54.4 %gather_fusion.2 = f32[16384,4]{1,0:T(8,128)} fusion(f32[4,768]{0,1:T(8,128)S(1)} %bitcast.254, s32[16384]{0:T(1024)S(1)} %broadcast_clamp_fusion.10), kind=kCustom, calls=%fused_computation.3.clone.clone.1 | custom fusion | bytes 589824 | tf_op jit(solution)/shard_map/while/body/eval_jaxpr/gather | solution.py:86
  465.8 54.4 %gather_fusion.2 = f32[16384,4]{1,0:T(8,128)} fusion(f32[4,768]{0,1:T(8,128)S(1)} %bitcast.254, s32[16384]{0:T(1024)S(1)} %broadcast_clamp_fusion.10), kind=kCustom, calls=%fused_computation.3.clone.clone.1 | custom fusion | bytes 589824 | tf_op jit(solution)/shard_map/while/body/eval_jaxpr/gather | solution.py:86
  527.4 54.4 %gather_fusion.2 = f32[16384,4]{1,0:T(8,128)} fusion(f32[4,768]{0,1:T(8,128)S(1)} %bitcast.254, s32[16384]{0:T(1024)S(1)} %broadcast_clamp_fusion.10), kind=kCustom, calls=%fused_computation.3.clone.clone.1 | custom fusion | bytes 589824 | tf_op jit(solution)/shard_map/while/body/eval_jaxpr/gather | solution.py:86
  589.0 54.4 %gather_fusion.2 = f32[16384,4]{1,0:T(8,128)} fusion(f32[4,768]{0,1:T(8,128)S(1)} %bitcast.254, s32[16384]{0:T(1024)S(1)} %broadcast_clamp_fusion.10), kind=kCustom, calls=%fused_computation.3.clone.clone.1 | custom fusion | bytes 589824 | tf_op jit(solution)/shard_map/while/body/eval_jaxpr/gather | solution.py:86
  649.9 8.5 all_gather.28
  659.7 9.1 all_gather.29
  676.0 246.4 %while.46 = (s32[]{:T(128)}, f32[4,3,512]{2,0,1:T(4,128)S(1)}, f32[4,4,768]{2,0,1:T(4,128)S(1)}, s32[32,512]{1,0:T(8,128)S(1)}, s32[]{:T(128)}, /*index=5*/s32[]{:T(128)}) while((s32[]{:T(128)}, f32[4,3,512]{2,0,1:T(4,128)S(1)}, f32[4,4,768]{2,0,1:T(4,128)S(1)}, s32[32,512]{1,0:T(8,128)S(1)}, s32[]{:T(128)}, ...), condition=%wide.region_18.19_spmd.clone, body=%wide.region_15.18_spmd.clone.sunk | while | flops 379906 | bytes 2381909 | solution.py:137
  677.7 54.4 %gather_fusion.4 = f32[16384,4]{1,0:T(8,128)} fusion(f32[4,768]{0,1:T(8,128)S(1)} %bitcast.256, s32[16384]{0:T(1024)S(1)} %broadcast_clamp_fusion.11), kind=kCustom, calls=%fused_computation.5.clone.clone.1 | custom fusion | bytes 589824 | tf_op jit(solution)/shard_map/while/body/eval_jaxpr/gather | solution.py:86
  739.3 54.4 %gather_fusion.4 = f32[16384,4]{1,0:T(8,128)} fusion(f32[4,768]{0,1:T(8,128)S(1)} %bitcast.256, s32[16384]{0:T(1024)S(1)} %broadcast_clamp_fusion.11), kind=kCustom, calls=%fused_computation.5.clone.clone.1 | custom fusion | bytes 589824 | tf_op jit(solution)/shard_map/while/body/eval_jaxpr/gather | solution.py:86
  800.9 54.4 %gather_fusion.4 = f32[16384,4]{1,0:T(8,128)} fusion(f32[4,768]{0,1:T(8,128)S(1)} %bitcast.256, s32[16384]{0:T(1024)S(1)} %broadcast_clamp_fusion.11), kind=kCustom, calls=%fused_computation.5.clone.clone.1 | custom fusion | bytes 589824 | tf_op jit(solution)/shard_map/while/body/eval_jaxpr/gather | solution.py:86
  862.5 54.4 %gather_fusion.4 = f32[16384,4]{1,0:T(8,128)} fusion(f32[4,768]{0,1:T(8,128)S(1)} %bitcast.256, s32[16384]{0:T(1024)S(1)} %broadcast_clamp_fusion.11), kind=kCustom, calls=%fused_computation.5.clone.clone.1 | custom fusion | bytes 589824 | tf_op jit(solution)/shard_map/while/body/eval_jaxpr/gather | solution.py:86
  940.7 23.1 %psum.15 = f32[4,3,768]{2,0,1:T(4,128)S(1)} all-reduce(f32[4,3,768]{2,0,1:T(4,128)S(1)} %fusion.66), channel_id=1, replica_groups=mesh['bead'=8,'space'=4] {'bead'}, use_global_device_ids=true, to_apply=%region_23.24 | all-reduce | flops 9216 | bytes 73728 | tf_op jit(solution)/shard_map/psum | solution.py:144
  964.7 27.7 %gather_fusion.15 = f32[8192,3]{1,0:T(8,128)} fusion(f32[3,768]{0,1:T(8,128)S(1)} %bitcast.294, s32[8192]{0:T(1024)S(1)} %broadcast_clamp_fusion.4), kind=kCustom, calls=%fused_computation.15 | custom fusion | bytes 229376 | tf_op jit(solution)/shard_map/gather | solution.py:97
  992.4 246.4 %while.47 = (s32[]{:T(128)}, f32[4,3,512]{2,0,1:T(4,128)S(1)}, f32[4,4,768]{2,0,1:T(4,128)S(1)}, s32[32,512]{1,0:T(8,128)S(1)}, s32[]{:T(128)}, /*index=5*/s32[]{:T(128)}) while((s32[]{:T(128)}, f32[4,3,512]{2,0,1:T(4,128)S(1)}, f32[4,4,768]{2,0,1:T(4,128)S(1)}, s32[32,512]{1,0:T(8,128)S(1)}, s32[]{:T(128)}, ...), condition=%wide.region_22.23_spmd.clone, body=%wide.region_19.22_spmd.clone.sunk | while | flops 379906 | bytes 2381909 | solution.py:137
  994.2 54.4 %gather_fusion.6 = f32[16384,4]{1,0:T(8,128)} fusion(f32[4,768]{0,1:T(8,128)S(1)} %bitcast.258, s32[16384]{0:T(1024)S(1)} %broadcast_clamp_fusion.12), kind=kCustom, calls=%fused_computation.7.clone.clone.1 | custom fusion | bytes 589824 | tf_op jit(solution)/shard_map/while/body/eval_jaxpr/gather | solution.py:86
  1055.8 54.4 %gather_fusion.6 = f32[16384,4]{1,0:T(8,128)} fusion(f32[4,768]{0,1:T(8,128)S(1)} %bitcast.258, s32[16384]{0:T(1024)S(1)} %broadcast_clamp_fusion.12), kind=kCustom, calls=%fused_computation.7.clone.clone.1 | custom fusion | bytes 589824 | tf_op jit(solution)/shard_map/while/body/eval_jaxpr/gather | solution.py:86
  1117.4 54.4 %gather_fusion.6 = f32[16384,4]{1,0:T(8,128)} fusion(f32[4,768]{0,1:T(8,128)S(1)} %bitcast.258, s32[16384]{0:T(1024)S(1)} %broadcast_clamp_fusion.12), kind=kCustom, calls=%fused_computation.7.clone.clone.1 | custom fusion | bytes 589824 | tf_op jit(solution)/shard_map/while/body/eval_jaxpr/gather | solution.py:86
  1179.0 54.4 %gather_fusion.6 = f32[16384,4]{1,0:T(8,128)} fusion(f32[4,768]{0,1:T(8,128)S(1)} %bitcast.258, s32[16384]{0:T(1024)S(1)} %broadcast_clamp_fusion.12), kind=kCustom, calls=%fused_computation.7.clone.clone.1 | custom fusion | bytes 589824 | tf_op jit(solution)/shard_map/while/body/eval_jaxpr/gather | solution.py:86
  1244.8 10.8 all_gather.31
  (411 shorter events, 181.3 us)
Async XLA Ops:
  0.6 361.2 %copy-start = (f32[128,8]{0,1:T(8,128)S(1)}, f32[128,8]{0,1:T(8,128)}, u32[]{:S(2)}) copy-start(f32[128,8]{0,1:T(8,128)} %param.31) | copy-start | bytes 12292
  4.5 17.3 %collective-permute-start = (f32[4,4,128]{2,0,1:T(4,128)S(1)}, f32[4,4,128]{2,0,1:T(4,128)S(1)}, u32[]{:S(2)}, u32[]{:S(2)}) collective-permute-start(f32[4,4,128]{2,0,1:T(4,128)S(1)} %get-tuple-element.258), channel_id=1, source_target_pairs={{0,1},{1,2},{2,3},{3,0},{4,5},{5,6},{6,7},{7,4},{8,9},{9,10},{10,1... | collective-permute-start | bytes 24584 | tf_op jit(solution)/shard_map/ppermute | solution.py:25
  7.6 14.2 %collective-permute-start.1 = (f32[4,4,128]{2,0,1:T(4,128)S(1)}, f32[4,4,128]{2,0,1:T(4,128)S(1)}, u32[]{:S(2)}, u32[]{:S(2)}) collective-permute-start(f32[4,4,128]{2,0,1:T(4,128)S(1)} %get-tuple-element.259), channel_id=1, source_target_pairs={{1,0},{2,1},{3,2},{0,3},{5,4},{6,5},{7,6},{4,7},{9,8},{10,9},{11,1... | collective-permute-start | bytes 24584 | tf_op jit(solution)/shard_map/ppermute | solution.py:28
  22.6 249.8 %copy-start.7 = (f32[4,32]{1,0:T(4,128)S(1)}, f32[4,32]{1,0:T(4,128)}, u32[]{:S(2)}) copy-start(f32[4,32]{1,0:T(4,128)} %constant.149.clone) | copy-start | bytes 1540
  296.6 61.6 %copy-start.1 = (s32[32,512]{1,0:T(8,128)S(1)}, s32[32,512]{1,0:T(8,128)}, u32[]{:S(2)}) copy-start(s32[32,512]{1,0:T(8,128)} %get-tuple-element.432) | copy-start | bytes 196612
  329.4 32.2 %copy-start.9 = (f32[8]{0:T(128)S(1)}, f32[8]{0:T(128)}, u32[]{:S(2)}) copy-start(f32[8]{0:T(128)} %constant.154) | copy-start | bytes 100
  329.5 32.8 %copy-start.8 = (f32[8,128]{1,0:T(8,128)S(1)}, f32[8,128]{1,0:T(8,128)}, u32[]{:S(2)}) copy-start(f32[8,128]{1,0:T(8,128)} %param.32) | copy-start | bytes 12292
  358.1 4.5 copy-start.3
  361.7 13.8 %copy-start.5 = (f32[4,3,512]{2,0,1:T(4,128)S(1)}, f32[4,3,512]{2,0,1:T(4,128)}, u32[]{:S(2)}) copy-start(f32[4,3,512]{2,0,1:T(4,128)} %param.25) | copy-start | bytes 73732
  361.7 23.3 %copy-start.6 = (f32[32,32]{1,0:T(8,128)S(1)}, f32[32,32]{1,0:T(8,128)}, u32[]{:S(2)}) copy-start(f32[32,32]{1,0:T(8,128)} %constant.146.clone) | copy-start | bytes 12292
  396.9 5.5 collective-permute-start.2
  397.0 5.4 collective-permute-start.3
  670.4 5.5 collective-permute-start.4
  670.5 5.5 collective-permute-start.5
  933.2 59.3 %copy-start.4 = (f32[4,3,512]{2,0,1:T(4,128)}, f32[4,3,512]{2,0,1:T(4,128)S(1)}, u32[]{:S(2)}) copy-start(f32[4,3,512]{2,0,1:T(4,128)S(1)} %fusion.18) | copy-start | bytes 73732
  934.8 5.6 collective-permute-start.6
  936.0 4.4 collective-permute-start.7
  1238.9 4.5 copy-start.2
where the time goes:
time: 1260 us
  local copies, waits for them, and re-layouts  1080 us (86%)
  blocking collectives  122 us (10%)
  other arithmetic  19.8 us (2%)
  starting transfers between devices  16.9 us (1%)
    gather x32, local copies, waits for them, and re-layouts, pair_forces(): others = extended[:, targets]  955 us
    gather x2, local copies, waits for them, and re-layouts, learned_forces(): others = extended[:, targets]  55.4 us
    psum x2, blocking collectives, expensive_forces(): extended = lax.psum(window_term, 'bead')  47 us
    gather x2, local copies, waits for them, and re-layouts, learned_forces(): weights = charges[targets] * live  32.9 us
    all_gather x3, blocking collectives, body(): lax.all_gather(coords, 'bead', axis=0, tiled=True)  27.6 us
    all_gather x3, blocking collectives, body(): lax.all_gather(moments, 'bead', axis=0, tiled=True)  25.6 us
  transfers between devices with their start and end apart: 8, of which 3 were waited for; matrix products, arithmetic and copies ran while one was open for 0% of the time, Pallas kernels for 0%

commit v1 on v0

v1 whole, which is shorter than its diff:
```python
import jax
import jax.numpy as jnp
import numpy as np
from jax import lax
from jax.experimental import pallas as pl
from jax.experimental.pallas import tpu as pltpu
from jax.sharding import PartitionSpec as P

BEADS = 32
CB = 4
NINNER = 3


polymer_freq = 10.0
outer_step = 6.0
pair_width = 1.0
pair_strength = 1.0
highest = lax.Precision.HIGHEST


def mode_matrix(count):
    beadpos = np.arange(count)[None, :]
    modeidx = np.arange(count)[:, None]
    middle = count // 2
    cosine = np.sqrt(2.0 / count) * np.cos(2.0 * np.pi * beadpos * modeidx / count)
    sine_rows = np.sqrt(2.0 / count) * np.sin(2.0 * np.pi * beadpos * modeidx / count)
    matrix = np.where(modeidx < middle, cosine, sine_rows)
    matrix = np.where(modeidx == 0, 1.0 / np.sqrt(count), matrix)
    matrix = np.where(modeidx == middle, np.cos(np.pi * beadpos) / np.sqrt(count), matrix)
    return matrix


def mode_scales(count, inner_step):
    frequency = 2.0 * polymer_freq * np.sin(np.pi * np.arange(count) / count)
    nonzero = np.where(frequency > 0, frequency, 1.0)
    cosine = np.cos(frequency * inner_step)
    drift_gain = np.where(frequency > 0, np.sin(frequency * inner_step) / nonzero, inner_step)
    spring = frequency * np.sin(frequency * inner_step)
    return (cosine, drift_gain, spring)


def contraction(count, fewer):
    full_modes = mode_matrix(count)
    small_modes = mode_matrix(fewer)
    kept = list(range(fewer // 2 + 1)) + list(range(count - fewer // 2 + 1, count))
    contract = np.sqrt(fewer / count) * (small_modes.T @ full_modes[kept])
    expand = count / fewer * contract.T
    return (contract, expand)


def radial_rates(count):
    return 0.2 * 2.0 ** (np.arange(count) / 2.0)

LANES = 128
TILE = 8
MESH = pl.DeviceIdType.MESH


def tables(devices, per_device):
    inner_step = outer_step / NINNER
    modes = mode_matrix(BEADS)
    cosine, drift_gain, spring = mode_scales(BEADS, inner_step)
    persist = modes.T @ (cosine[:, None] * modes)
    coupling = modes.T @ (drift_gain[:, None] * modes)
    restoring = -(modes.T @ (spring[:, None] * modes))
    contract, expand = contraction(BEADS, CB)
    rows = -(-6 * per_device // TILE) * TILE
    full = devices * rows
    blocks = ((persist, coupling), (restoring, persist))

    def places(component, kind):
        bead = np.arange(BEADS)
        local = component * 2 * per_device + kind * per_device + bead % per_device
        return bead // per_device * rows + local

    move = np.zeros((full, full))
    reduce = np.zeros((CB, TILE, full))
    spread = np.zeros((full, CB * TILE))
    for component in range(3):
        for out in range(2):
            for kind in range(2):
                move[np.ix_(places(component, out), places(component, kind))] = blocks[out][kind]
        for member in range(CB):
            reduce[member, component, places(component, 0)] = contract[member]
            spread[places(component, 1), member * TILE + component] = (
                0.5 * outer_step * expand[:, member]
            )
    reduce_moved = reduce @ move
    move_spread = move @ spread
    share = reduce.reshape(CB * TILE, devices, rows).transpose(1, 0, 2)
    found = (
        move.reshape(devices, rows, full),
        share,
        reduce_moved,
        spread.reshape(devices, rows, CB * TILE),
        move_spread.reshape(devices, rows, CB * TILE),
    )
    return tuple(jnp.asarray(table, jnp.float32) for table in found)


def dot(a, b):
    return jnp.dot(a, b, precision=highest, preferred_element_type=jnp.float32)


def pick(chunks, low, high):
    found = None
    for number, chunk in enumerate(chunks):
        value = jnp.take_along_axis(chunk, low, axis=1, mode="promise_in_bounds")
        found = value if found is None else jnp.where(high == number, value, found)
    return found


def cycle_kernel(
    pos_ref, mom_ref, near_ref, ghost_ref, species_ref, scale_ref, mass_ref, w_in_ref, w_out_ref,
    move_ref, share_ref, moved_ref, spread_ref, mspread_ref,
    new_pos_ref, new_mom_ref,
    state, kick, weight, gathered, ghost_out, ghost_in, part_out, part_in, whole,
    qghost_out, qghost_in, piece,
    part_s, part_r, ghost_s, ghost_r, qghost_s, qghost_r, all_s, all_r, piece_s, piece_r,
):
    per_device, _, atoms = pos_ref.shape
    slots = near_ref.shape[0]
    rows = state.shape[1]
    ghosts = ghost_ref.shape[1]
    devices = lax.axis_size("bead")
    domains = lax.axis_size("space")
    me = lax.axis_index("bead")
    domain = lax.axis_index("space")
    above = lax.rem(domain + 1, domains)
    below = lax.rem(domain + domains - 1, domains)
    peers = [lax.rem(me + j, devices) for j in range(devices)]
    senders = [lax.rem(me + devices - j, devices) for j in range(devices)]
    inner_step = outer_step / NINNER
    groups = devices // CB
    share = atoms // groups
    cover = piece.shape[3]
    member = me // groups
    first = lax.rem(me, groups) * share // LANES * LANES
    ghost_chunks = ghosts // LANES
    atom_chunks = atoms // LANES

    barrier = pltpu.get_barrier_semaphore()
    for j in range(1, devices):
        pl.semaphore_signal(barrier, inc=1, device_id={"bead": peers[j]}, device_id_type=MESH)
    for target in (above, below):
        pl.semaphore_signal(barrier, inc=1, device_id={"space": target}, device_id_type=MESH)

    def to_peer(src, dst, send, recv, j):
        return pltpu.make_async_remote_copy(
            src_ref=src, dst_ref=dst, send_sem=send.at[j], recv_sem=recv.at[j],
            device_id={"bead": peers[j]}, device_id_type=MESH,
        )

    def to_side(src, dst, send, recv, side):
        return pltpu.make_async_remote_copy(
            src_ref=src, dst_ref=dst, send_sem=send.at[side], recv_sem=recv.at[side],
            device_id={"space": (above, below)[side]}, device_id_type=MESH,
        )

    def row_of(component, kind, bead):
        return (component * 2 + kind) * per_device + bead

    species = species_ref[...]
    charge = jnp.zeros((1, atoms), jnp.float32)
    mass = jnp.zeros((1, atoms), jnp.float32)
    for kind in range(scale_ref.shape[0]):
        charge = jnp.where(species == kind, scale_ref[kind], charge)
        mass = jnp.where(species == kind, mass_ref[kind], mass)
    inverse = 1.0 / mass

    kick[...] = jnp.zeros(kick.shape, jnp.float32)
    if rows > 6 * per_device:
        state[0] = jnp.zeros((rows, atoms), jnp.float32)
    for component in range(3):
        for bead in range(per_device):
            at = row_of(component, 0, bead)
            state[0, at : at + 1, :] = pos_ref[bead, component : component + 1, :]
            at = row_of(component, 1, bead)
            state[0, at : at + 1, :] = mom_ref[bead, component : component + 1, :] * inverse

    def ghost_rows_of(block, side):
        chunks = [block[:, m * LANES : (m + 1) * LANES] for m in range(atom_chunks)]
        parts = []
        for g in range(ghost_chunks):
            index = ghost_ref[1 - side : 2 - side, g * LANES : (g + 1) * LANES]
            index = jnp.broadcast_to(index, (TILE, LANES))
            parts.append(pick(chunks, index & (LANES - 1), index // LANES))
        return parts

    def send_ghosts(step, extra):
        for side in range(2):
            for tile in range(rows // TILE + 1):
                at = tile * TILE
                block = extra if tile == rows // TILE else state[step, at : at + TILE, :]
                if block is None:
                    block = jnp.zeros((TILE, atoms), jnp.float32)
                for g, part in enumerate(ghost_rows_of(block, side)):
                    ghost_out[step, side, at : at + TILE, g * LANES : (g + 1) * LANES] = part
        return [
            to_side(ghost_out.at[step, side], ghost_in.at[step, side],
                    ghost_s.at[step], ghost_r.at[step], side)
            for side in range(2)
        ]

    def spread_row(row):
        return jnp.broadcast_to(row, (TILE, LANES))

    def ghost_window(buffer, lead, row):
        def parts(side):
            return [
                spread_row(buffer[(*lead, side, slice(row, row + 1), slice(g * LANES, (g + 1) * LANES))])
                for g in range(ghost_chunks)
            ]
        return parts(0), parts(1)

    def window_of(step, row):
        low, high = ghost_window(ghost_in, (step,), row)
        own = [
            spread_row(state[step, row : row + 1, m * LANES : (m + 1) * LANES])
            for m in range(atom_chunks)
        ]
        return low + own + high

    def cheap(step):
        @pl.loop(0, atom_chunks)
        def _(j):
            lanes = pl.ds(pl.multiple_of(j * LANES, LANES), LANES)
            factor = whole[1, 0:1, lanes]
            indices = [near_ref[k : k + TILE, lanes] for k in range(0, slots, TILE)]
            lows = [index & (LANES - 1) for index in indices]
            highs = [index // LANES for index in indices]
            for bead in range(per_device):
                offsets = []
                for component in range(3):
                    row = row_of(component, 0, bead)
                    chunks = window_of(step, row)
                    middle = spread_row(state[step, row : row + 1, lanes])
                    offsets.append(
                        [pick(chunks, low, high) - middle for low, high in zip(lows, highs)]
                    )
                totals = [None] * 3
                for t in range(len(indices)):
                    squared = sum(offsets[c][t] * offsets[c][t] for c in range(3))
                    strength = weight[t * TILE : (t + 1) * TILE, lanes] * jnp.exp(
                        -squared / pair_width
                    )
                    for c in range(3):
                        term = strength * offsets[c][t]
                        totals[c] = term if totals[c] is None else totals[c] + term
                for c in range(3):
                    row = row_of(c, 1, bead)
                    total = jnp.sum(totals[c], axis=0, keepdims=True)
                    kick[row : row + 1, lanes] = pair_strength * factor * total

    def learned(low_high, slot):
        rates = radial_rates(w_in_ref.shape[1])
        for t in range(cover // LANES):
            lanes = pl.ds(pl.multiple_of(first + t * LANES, LANES), LANES)
            indices = [near_ref[k : k + TILE, lanes] for k in range(0, slots, TILE)]
            offsets = []
            for c in range(3):
                low, high = low_high(c)
                own = [
                    spread_row(whole[0, c : c + 1, m * LANES : (m + 1) * LANES])
                    for m in range(atom_chunks)
                ]
                chunks = low + own + high
                middle = spread_row(whole[0, c : c + 1, lanes])
                offsets.append(
                    [pick(chunks, index & (LANES - 1), index // LANES) - middle for index in indices]
                )
            bases = []
            messages = [None] * len(rates)
            for k in range(len(indices)):
                squared = sum(offsets[c][k] * offsets[c][k] for c in range(3))
                basis = [jnp.exp(-float(rates[r]) * squared) for r in range(2)]
                for r in range(2, len(rates)):
                    basis.append(basis[r - 2] * basis[r - 2])
                bases.append(basis)
                strength = weight[k * TILE : (k + 1) * TILE, lanes]
                for r in range(len(rates)):
                    term = strength * basis[r]
                    messages[r] = term if messages[r] is None else messages[r] + term
            message = jnp.concatenate(
                [jnp.sum(m, axis=0, keepdims=True) for m in messages], axis=0
            ) / slots
            hidden = dot(w_in_ref[...], message)
            hidden = hidden * jax.nn.sigmoid(hidden)
            radial = dot(w_out_ref[...], hidden)
            spread_radial = [spread_row(radial[r : r + 1, :]) for r in range(len(rates))]
            totals = [None] * 3
            for k in range(len(indices)):
                profile = sum(spread_radial[r] * bases[k][r] for r in range(len(rates)))
                strength = weight[k * TILE : (k + 1) * TILE, lanes] * profile
                for c in range(3):
                    term = strength * offsets[c][k]
                    totals[c] = term if totals[c] is None else totals[c] + term
            which = lax.broadcasted_iota(jnp.int32, (TILE, LANES), 0)
            tile = jnp.zeros((TILE, LANES), jnp.float32)
            for c in range(3):
                total = spread_row(jnp.sum(totals[c], axis=0, keepdims=True))
                tile = jnp.where(which == c, total, tile)
            piece[slot, me, :, t * LANES : (t + 1) * LANES] = tile

    def send_piece(slot):
        return [
            to_peer(piece.at[slot, me], piece.at[slot, me], piece_s.at[slot], piece_r.at[slot], j)
            for j in range(1, devices)
        ]

    def await_blocks(buffer, send, recv):
        for j in range(1, devices):
            to_peer(buffer.at[senders[j]], buffer.at[senders[j]], send, recv, j).wait_recv()

    def all_pieces(slot):
        parts = []
        for c in range(CB):
            line = []
            for m in range(atom_chunks):
                source = c * groups + m * LANES // share
                start = m * LANES - (source % groups) * share // LANES * LANES
                line.append(piece[slot, source, :, start : start + LANES])
            parts.append(jnp.concatenate(line, axis=1))
        return jnp.concatenate(parts, axis=0)

    sent = []

    def start(copies):
        for copy in copies:
            copy.start()
            sent.append(copy)

    parts = dot(share_ref[me], state[0])
    for c in range(CB):
        part_out[c] = parts[c * TILE : (c + 1) * TILE, :]
    copies = [
        to_peer(part_out.at[peers[j] // groups], part_in.at[me], part_s, part_r, j)
        for j in range(1, devices)
    ]
    ghost_copies = send_ghosts(0, jnp.broadcast_to(charge, (TILE, atoms)))
    whole[1] = jnp.broadcast_to(charge * inverse, (TILE, atoms))

    pl.semaphore_wait(barrier, devices + 1)
    start(copies)
    start(ghost_copies)
    await_blocks(part_in, part_s, part_r)
    contracted = part_out[member]
    for j in range(1, devices):
        contracted = contracted + part_in[senders[j]]
    whole[0] = contracted
    for side in range(2):
        for g, part in enumerate(ghost_rows_of(contracted, side)):
            qghost_out[side, :, g * LANES : (g + 1) * LANES] = part
    qcopies = [
        to_side(qghost_out.at[side], qghost_in.at[side], qghost_s, qghost_r, side)
        for side in range(2)
    ]
    start(qcopies)
    for copy in ghost_copies:
        copy.wait_recv()

    low, high = ghost_window(ghost_in, (0,), rows)
    own = [spread_row(charge[:, m * LANES : (m + 1) * LANES]) for m in range(atom_chunks)]
    chunks = low + own + high
    for m in range(atom_chunks):
        lanes = slice(m * LANES, (m + 1) * LANES)
        itself = ghosts + m * LANES + lax.broadcasted_iota(jnp.int32, (TILE, LANES), 1)
        for k in range(0, slots, TILE):
            index = near_ref[k : k + TILE, lanes]
            value = pick(chunks, index & (LANES - 1), index // LANES)
            weight[k : k + TILE, lanes] = jnp.where(index == itself, 0.0, value)

    cheap(0)
    gathered[0, me] = state[0] + (0.5 * inner_step) * kick[...]
    start([
        to_peer(gathered.at[0, me], gathered.at[0, me], all_s.at[0], all_r.at[0], j)
        for j in range(1, devices)
    ])
    for copy in qcopies:
        copy.wait_recv()
    learned(lambda c: ghost_window(qghost_in, (), c), 0)
    start(send_piece(0))
    await_blocks(gathered.at[0], all_s.at[0], all_r.at[0])
    await_blocks(piece.at[0], piece_s.at[0], piece_r.at[0])

    for step in range(1, NINNER + 1):
        every = gathered[step - 1].reshape(devices * rows, atoms)
        fresh = dot(move_ref[me], every)
        if step == 1:
            fresh = fresh + dot(mspread_ref[me], all_pieces(0) * inverse)
        state[step] = fresh
        extra = None
        if step == NINNER:
            extra = dot(moved_ref[member], every)
            whole[0] = extra
        ghost_copies = send_ghosts(step, extra)
        start(ghost_copies)
        for copy in ghost_copies:
            copy.wait_recv()
        if step == NINNER:
            learned(lambda c: ghost_window(ghost_in, (step,), rows + c), 1)
            start(send_piece(1))
        cheap(step)
        if step < NINNER:
            gathered[step, me] = state[step] + inner_step * kick[...]
            start([
                to_peer(gathered.at[step, me], gathered.at[step, me],
                        all_s.at[step], all_r.at[step], j)
                for j in range(1, devices)
            ])
            await_blocks(gathered.at[step], all_s.at[step], all_r.at[step])

    await_blocks(piece.at[1], piece_s.at[1], piece_r.at[1])
    kick[...] = (state[NINNER] + (0.5 * inner_step) * kick[...]) * mass + dot(
        spread_ref[me], all_pieces(1)
    )
    for component in range(3):
        for bead in range(per_device):
            at = row_of(component, 0, bead)
            new_pos_ref[bead, component : component + 1, :] = state[NINNER, at : at + 1, :]
            at = row_of(component, 1, bead)
            new_mom_ref[bead, component : component + 1, :] = kick[at : at + 1, :]
    for copy in sent:
        copy.wait_send()


def body(
    positions, momenta, neighbours, ghost_rows, species, species_scale, mass_table, w_in, w_out
):
    per_device, _, atoms = positions.shape
    slots = neighbours.shape[0]
    ghosts = ghost_rows.shape[0] // 2
    devices = lax.axis_size("bead")
    consts = tables(devices, per_device)
    rows = consts[0].shape[1]
    cover = max(atoms // (devices // CB), LANES)
    vmem = pl.BlockSpec(memory_space=pltpu.VMEM)
    smem = pl.BlockSpec(memory_space=pltpu.SMEM)
    f32 = jnp.float32
    dma = pltpu.SemaphoreType.DMA
    shape = jax.ShapeDtypeStruct(positions.shape, f32)
    return pl.pallas_call(
        cycle_kernel,
        name="cycle",
        out_shape=(shape, shape),
        in_specs=[vmem] * 5 + [smem] * 2 + [vmem] * 7,
        out_specs=(vmem, vmem),
        scratch_shapes=[
            pltpu.VMEM((NINNER + 1, rows, atoms), f32),
            pltpu.VMEM((rows, atoms), f32),
            pltpu.VMEM((slots, atoms), f32),
            pltpu.VMEM((NINNER, devices, rows, atoms), f32),
            pltpu.VMEM((NINNER + 1, 2, rows + TILE, ghosts), f32),
            pltpu.VMEM((NINNER + 1, 2, rows + TILE, ghosts), f32),
            pltpu.VMEM((CB, TILE, atoms), f32),
            pltpu.VMEM((devices, TILE, atoms), f32),
            pltpu.VMEM((2, TILE, atoms), f32),
            pltpu.VMEM((2, TILE, ghosts), f32),
            pltpu.VMEM((2, TILE, ghosts), f32),
            pltpu.VMEM((2, devices, TILE, cover), f32),
            dma((devices,)), dma((devices,)),
            dma((NINNER + 1, 2)), dma((NINNER + 1, 2)),
            dma((2,)), dma((2,)),
            dma((NINNER, devices)), dma((NINNER, devices)),
            dma((2, devices)), dma((2, devices)),
        ],
        compiler_params=pltpu.CompilerParams(
            collective_id=0, has_side_effects=True, vmem_limit_bytes=32 * 1024 * 1024
        ),
    )(
        positions, momenta, neighbours, ghost_rows.reshape(2, ghosts), species.reshape(1, atoms),
        species_scale, mass_table, w_in, w_out, *consts,
    )


def solution(mesh):
    in_specs = (
        P("bead", None, "space"),
        P("bead", None, "space"),
        P(None, "space"),
        P("space"),
        P("space"),
        P(),
        P(),
        P(),
        P(),
    )
    out_specs = (P("bead", None, "space"), P("bead", None, "space"))
    return jax.shard_map(body, mesh=mesh, in_specs=in_specs, out_specs=out_specs, check_vma=False)
```

time: 1260 us -> 60.6 us (0.05)
  local copies, waits for them, and re-layouts: 1080 us -> 7.18 us
  blocking collectives: 122 us -> 0 us
  Pallas kernels: 0 us -> 52.3 us
  other arithmetic: 19.8 us -> 0 us
  starting transfers between devices: 16.9 us -> 0 us
    gather x62 -> x0, local copies, waits for them, and re-layouts: 1070 us -> none  [the longest x32 955 us: pair_forces(): others = extended[:, targets]]
    all_gather x8 -> x0, blocking collectives: 75.1 us -> none  [the longest x3 27.6 us: body(): lax.all_gather(coords, 'bead', axis=0, tiled=True)]
    pallas_call x0 -> x1, Pallas kernels: none -> 52.3 us  [body(): pl.pallas_call(cycle_kernel, name='cycle', out_shape=(shape, shape), in_s...]
    psum x2 -> x0, blocking collectives: 47 us -> none  [expensive_forces(): extended = lax.psum(window_term, 'bead')]
    ppermute x8 -> x0, starting transfers between devices: 16.9 us -> none  [the longest x4 12.6 us: with_halo(): lax.ppermute(lax.slice_in_dim(block, 0, width, axis=dim), axis, backward)]
  transfers between devices with their start and end apart: 8 -> 0, of which waited for: 3 -> 0; matrix products, arithmetic and copies ran while one was open for 0% -> 0% of each run, Pallas kernels for 0% -> 0%
where the time goes in v1:
time: 60.6 us; the launch traced here: 60.2 us
  Pallas kernels  52.3 us (86%)
  local copies, waits for them, and re-layouts  7.18 us (12%)
  between operations  0.76 us (1%)
    pallas_call x1, Pallas kernels, body(): pl.pallas_call(cycle_kernel, name='cycle', out_shape=(shape, shape), in_s...  52.3 us
    unnamed x25, local copies, waits for them, and re-layouts  5.94 us
    pallas_call x2, local copies, waits for them, and re-layouts, body(): pl.pallas_call(cycle_kernel, name='cycle', out_shape=(shape, shape), in_s...  1.24 us

profile of v1, /device:TPU:0, one launch (start us, length us, event | category | flops | bytes accessed | tf_op | source)
XLA Modules:
  0.0 60.2 jit_solution(8837084013308382079)
XLA Ops:
  0.6 0.0 copy-start.1
  0.6 0.8 %copy.16.pos_ref = f32[4,3,512]{2,1,0:T(4,128)S(1)} copy(f32[4,3,512]{2,0,1:T(4,128)} %param.14) | data formatting | bytes 49152 | tf_op args[0]
  1.4 0.8 %copy.17.mom_ref = f32[4,3,512]{2,1,0:T(4,128)S(1)} copy(f32[4,3,512]{2,0,1:T(4,128)} %param.15) | data formatting | bytes 49152 | tf_op args[1]
  2.2 0.0 copy-start.5
  2.2 0.0 copy-start.6
  2.2 0.0 copy-start.7
  2.2 0.0 copy-start.8
  2.2 0.0 copy-start.9
  2.2 0.0 copy-start.10
  2.3 0.8 %copy.18.w_in_ref = f32[128,8]{1,0:T(8,128)S(1)} copy(f32[128,8]{0,1:T(8,128)} %param.21) | data formatting | bytes 8192 | tf_op args[7]
  3.1 0.0 copy-done.1
  3.1 0.0 copy-done.5
  3.1 0.0 copy-done.6
  3.1 0.0 copy-done.7
  3.1 0.0 copy-done.8
  3.1 0.0 copy-done.9
  3.1 0.0 copy-done.10
  3.1 0.0 copy-start
  3.1 0.9 %copy-done = f32[8,24,192]{2,1,0:T(8,128)S(1)} copy-done((f32[8,24,192]{2,1,0:T(8,128)S(1)}, f32[8,24,192]{2,1,0:T(8,128)}, u32[]{:S(2)}) %copy-start) | copy-done | bytes 147480
  4.1 0.0 copy-start.2
  4.1 0.9 %copy-done.2 = f32[8,24,32]{2,1,0:T(8,128)S(1)} copy-done((f32[8,24,32]{2,1,0:T(8,128)S(1)}, f32[8,24,32]{2,1,0:T(8,128)}, u32[]{:S(2)}) %copy-start.2) | copy-done | bytes 24600
  5.0 0.0 copy-start.3
  5.0 0.9 %copy-done.3 = f32[8,24,32]{2,1,0:T(8,128)S(1)} copy-done((f32[8,24,32]{2,1,0:T(8,128)S(1)}, f32[8,24,32]{2,1,0:T(8,128)}, u32[]{:S(2)}) %copy-start.3) | copy-done | bytes 24600
  5.9 0.0 copy-start.4
  5.9 0.8 %copy-done.4 = s32[32,512]{1,0:T(8,128)S(1)} copy-done((s32[32,512]{1,0:T(8,128)S(1)}, s32[32,512]{1,0:T(8,128)}, u32[]{:S(2)}) %copy-start.4) | copy-done | bytes 65560
  6.7 52.3 %cycle.1 = (f32[4,3,512]{2,1,0:T(4,128)S(1)}, f32[4,3,512]{2,1,0:T(4,128)S(1)}) custom-call(f32[4,3,512]{2,1,0:T(4,128)S(1)} %copy.16.pos_ref, f32[4,3,512]{2,1,0:T(4,128)S(1)} %copy.17.mom_ref, s32[32,512]{1,0:T(8,128)S(1)} %copy-done.4, s32[2,128]{1,0:T(2,128)S(1)} %bitcast.3, s32[1,512]{1,0:T(1,128)S(1)} %bitcast.2, f32[2]{0:T(128)S(1)} %copy-done.9, ...), custom_call_target="tpu_custom_call" | custom-call | tf_op jit(solution)/shard_map/cycle/pallas_call | solution.py:442
  59.0 0.6 %copy.19 = f32[4,3,512]{2,0,1:T(4,128)} copy(f32[4,3,512]{2,1,0:T(4,128)S(1)} %get-tuple-element.2) | data formatting | bytes 49152 | tf_op jit(solution)/shard_map/cycle/pallas_call | solution.py:442
  59.6 0.6 %copy.20 = f32[4,3,512]{2,0,1:T(4,128)} copy(f32[4,3,512]{2,1,0:T(4,128)S(1)} %get-tuple-element.3) | data formatting | bytes 49152 | tf_op jit(solution)/shard_map/cycle/pallas_call | solution.py:442
Async XLA Ops:
  0.6 2.4 %copy-start.1 = (f32[8,32,24]{2,1,0:T(8,128)S(1)}, f32[8,32,24]{2,1,0:T(8,128)}, u32[]{:S(2)}) copy-start(f32[8,32,24]{2,1,0:T(8,128)} %constant.11.clone.share_ref) | copy-start | bytes 73732
  2.2 0.9 %copy-start.5 = (f32[4,8,192]{2,1,0:T(8,128)S(1)}, f32[4,8,192]{2,1,0:T(8,128)}, u32[]{:S(2)}) copy-start(f32[4,8,192]{2,1,0:T(8,128)} %constant.12.clone.moved_ref) | copy-start | bytes 73732
  2.2 0.9 %copy-start.6 = (f32[8,128]{1,0:T(8,128)S(1)}, f32[8,128]{1,0:T(8,128)}, u32[]{:S(2)}) copy-start(f32[8,128]{1,0:T(8,128)} %w_out_ref.1) | copy-start | bytes 12292
  2.2 0.9 %copy-start.7 = (s32[512]{0:T(512)S(1)}, s32[512]{0:T(512)}, u32[]{:S(2)}) copy-start(s32[512]{0:T(512)} %param.18) | copy-start | bytes 6148
  2.2 0.9 %copy-start.8 = (s32[256]{0:T(256)S(1)}, s32[256]{0:T(256)}, u32[]{:S(2)}) copy-start(s32[256]{0:T(256)} %param.17) | copy-start | bytes 3076
  2.2 0.9 %copy-start.9 = (f32[2]{0:T(128)S(1)}, f32[2]{0:T(128)}, u32[]{:S(2)}) copy-start(f32[2]{0:T(128)} %scale_ref.1) | copy-start | bytes 28
  2.2 0.9 %copy-start.10 = (f32[2]{0:T(128)S(1)}, f32[2]{0:T(128)}, u32[]{:S(2)}) copy-start(f32[2]{0:T(128)} %mass_ref.1) | copy-start | bytes 28
  3.1 0.9 %copy-start = (f32[8,24,192]{2,1,0:T(8,128)S(1)}, f32[8,24,192]{2,1,0:T(8,128)}, u32[]{:S(2)}) copy-start(f32[8,24,192]{2,1,0:T(8,128)} %constant.10.clone.move_ref) | copy-start | bytes 442372
  4.1 0.9 %copy-start.2 = (f32[8,24,32]{2,1,0:T(8,128)S(1)}, f32[8,24,32]{2,1,0:T(8,128)}, u32[]{:S(2)}) copy-start(f32[8,24,32]{2,1,0:T(8,128)} %constant.14.clone.mspread_ref) | copy-start | bytes 73732
  5.0 0.9 %copy-start.3 = (f32[8,24,32]{2,1,0:T(8,128)S(1)}, f32[8,24,32]{2,1,0:T(8,128)}, u32[]{:S(2)}) copy-start(f32[8,24,32]{2,1,0:T(8,128)} %constant.13.clone.spread_ref) | copy-start | bytes 73732
  5.9 0.8 %copy-start.4 = (s32[32,512]{1,0:T(8,128)S(1)}, s32[32,512]{1,0:T(8,128)}, u32[]{:S(2)}) copy-start(s32[32,512]{1,0:T(8,128)} %near_ref.1) | copy-start | bytes 196612

commit v2 on v1

--- a/solution.py
+++ b/solution.py
@@ -85,17 +85,17 @@
             spread[places(component, 1), member * TILE + component] = (
                 0.5 * outer_step * expand[:, member]
             )
-    reduce_moved = reduce @ move
-    move_spread = move @ spread
+    reduce_moved = np.repeat(reduce @ move, devices // CB, axis=0)
+    move_spread = (move @ spread).reshape(devices, rows, CB * TILE)
     share = reduce.reshape(CB * TILE, devices, rows).transpose(1, 0, 2)
-    found = (
-        move.reshape(devices, rows, full),
-        share,
-        reduce_moved,
-        spread.reshape(devices, rows, CB * TILE),
-        move_spread.reshape(devices, rows, CB * TILE),
-    )
-    return tuple(jnp.asarray(table, jnp.float32) for table in found)
+    spread = spread.reshape(devices, rows, CB * TILE)
+    move = np.concatenate((move.reshape(devices, rows, full), move_spread), axis=2)
+
+    def padded(table):
+        return np.pad(table, ((0, 0), (0, 0), (0, move.shape[2] - table.shape[2])))
+
+    stacked = (move, padded(reduce_moved), padded(spread), padded(share))
+    return jnp.asarray(np.concatenate(stacked, axis=1), jnp.float32)
 
 
 def dot(a, b):
@@ -111,14 +111,15 @@
 
 
 def cycle_kernel(
-    pos_ref, mom_ref, near_ref, ghost_ref, species_ref, scale_ref, mass_ref, w_in_ref, w_out_ref,
-    move_ref, share_ref, moved_ref, spread_ref, mspread_ref,
+    pos_in, mom_in, near_in, ghost_from, species_in, scale_in, mass_in, w_in_in, w_out_in, table_in,
     new_pos_ref, new_mom_ref,
     state, kick, weight, gathered, ghost_out, ghost_in, part_out, part_in, whole,
     qghost_out, qghost_in, piece,
+    pos_ref, mom_ref, near_ref, ghost_ref, species_ref, scale_ref, mass_ref, w_in_ref, w_out_ref,
+    table_ref, load_s,
     part_s, part_r, ghost_s, ghost_r, qghost_s, qghost_r, all_s, all_r, piece_s, piece_r,
 ):
-    per_device, _, atoms = pos_ref.shape
+    _, per_device, atoms = pos_ref.shape
     slots = near_ref.shape[0]
     rows = state.shape[1]
     ghosts = ghost_ref.shape[1]
@@ -139,6 +140,16 @@
     ghost_chunks = ghosts // LANES
     atom_chunks = atoms // LANES
 
+    loads = [
+        pltpu.make_async_copy(src, dst, load_s.at[number])
+        for number, (src, dst) in enumerate((
+            (pos_in, pos_ref), (mom_in, mom_ref), (species_in, species_ref), (scale_in, scale_ref),
+            (mass_in, mass_ref), (table_in.at[me], table_ref), (ghost_from, ghost_ref),
+            (near_in, near_ref), (w_in_in, w_in_ref), (w_out_in, w_out_ref),
+        ))
+    ]
+    for load in loads:
+        load.start()
     barrier = pltpu.get_barrier_semaphore()
     for j in range(1, devices):
         pl.semaphore_signal(barrier, inc=1, device_id={"bead": peers[j]}, device_id_type=MESH)
@@ -160,23 +171,28 @@
     def row_of(component, kind, bead):
         return (component * 2 + kind) * per_device + bead
 
+    full = devices * rows
+    moved_row = rows
+    spread_row_at = moved_row + TILE
+    share_row = spread_row_at + rows
+    for load in loads:
+        load.wait()
     species = species_ref[...]
     charge = jnp.zeros((1, atoms), jnp.float32)
     mass = jnp.zeros((1, atoms), jnp.float32)
-    for kind in range(scale_ref.shape[0]):
-        charge = jnp.where(species == kind, scale_ref[kind], charge)
-        mass = jnp.where(species == kind, mass_ref[kind], mass)
+    for kind in range(scale_ref.shape[1]):
+        charge = jnp.where(species == kind, scale_ref[0:1, kind : kind + 1], charge)
+        mass = jnp.where(species == kind, mass_ref[0:1, kind : kind + 1], mass)
     inverse = 1.0 / mass
 
     kick[...] = jnp.zeros(kick.shape, jnp.float32)
     if rows > 6 * per_device:
         state[0] = jnp.zeros((rows, atoms), jnp.float32)
     for component in range(3):
-        for bead in range(per_device):
-            at = row_of(component, 0, bead)
-            state[0, at : at + 1, :] = pos_ref[bead, component : component + 1, :]
-            at = row_of(component, 1, bead)
-            state[0, at : at + 1, :] = mom_ref[bead, component : component + 1, :] * inverse
+        at = row_of(component, 0, 0)
+        state[0, at : at + per_device, :] = pos_ref[component]
+        at = row_of(component, 1, 0)
+        state[0, at : at + per_device, :] = mom_ref[component] * inverse
 
     def ghost_rows_of(block, side):
         chunks = [block[:, m * LANES : (m + 1) * LANES] for m in range(atom_chunks)]
@@ -253,7 +269,7 @@
                     kick[row : row + 1, lanes] = pair_strength * factor * total
 
     def learned(low_high, slot):
-        rates = radial_rates(w_in_ref.shape[1])
+        rates = radial_rates(w_in_ref.shape[0])
         for t in range(cover // LANES):
             lanes = pl.ds(pl.multiple_of(first + t * LANES, LANES), LANES)
             indices = [near_ref[k : k + TILE, lanes] for k in range(0, slots, TILE)]
@@ -284,7 +300,10 @@
             message = jnp.concatenate(
                 [jnp.sum(m, axis=0, keepdims=True) for m in messages], axis=0
             ) / slots
-            hidden = dot(w_in_ref[...], message)
+            hidden = lax.dot_general(
+                w_in_ref[...], message, (((0,), (0,)), ((), ())),
+                precision=highest, preferred_element_type=jnp.float32,
+            )
             hidden = hidden * jax.nn.sigmoid(hidden)
             radial = dot(w_out_ref[...], hidden)
             spread_radial = [spread_row(radial[r : r + 1, :]) for r in range(len(rates))]
@@ -330,7 +349,7 @@
             copy.start()
             sent.append(copy)
 
-    parts = dot(share_ref[me], state[0])
+    parts = dot(table_ref[share_row : share_row + CB * TILE, 0:rows], state[0])
     for c in range(CB):
         part_out[c] = parts[c * TILE : (c + 1) * TILE, :]
     copies = [
@@ -385,14 +404,18 @@
 
     for step in range(1, NINNER + 1):
         every = gathered[step - 1].reshape(devices * rows, atoms)
-        fresh = dot(move_ref[me], every)
+        extra = None
         if step == 1:
-            fresh = fresh + dot(mspread_ref[me], all_pieces(0) * inverse)
+            every = jnp.concatenate((every, all_pieces(0) * inverse), axis=0)
+            fresh = dot(table_ref[0:rows, :], every)
+        elif step < NINNER:
+            fresh = dot(table_ref[0:rows, 0:full], every)
+        else:
+            both = dot(table_ref[0 : moved_row + TILE, 0:full], every)
+            fresh = both[0:rows]
+            extra = both[moved_row:]
+            whole[0] = extra
         state[step] = fresh
-        extra = None
-        if step == NINNER:
-            extra = dot(moved_ref[member], every)
-            whole[0] = extra
         ghost_copies = send_ghosts(step, extra)
         start(ghost_copies)
         for copy in ghost_copies:
@@ -412,14 +435,13 @@
 
     await_blocks(piece.at[1], piece_s.at[1], piece_r.at[1])
     kick[...] = (state[NINNER] + (0.5 * inner_step) * kick[...]) * mass + dot(
-        spread_ref[me], all_pieces(1)
+        table_ref[spread_row_at : spread_row_at + rows, 0 : CB * TILE], all_pieces(1)
     )
     for component in range(3):
-        for bead in range(per_device):
-            at = row_of(component, 0, bead)
-            new_pos_ref[bead, component : component + 1, :] = state[NINNER, at : at + 1, :]
-            at = row_of(component, 1, bead)
-            new_mom_ref[bead, component : component + 1, :] = kick[at : at + 1, :]
+        at = row_of(component, 0, 0)
+        new_pos_ref[component] = state[NINNER, at : at + per_device, :]
+        at = row_of(component, 1, 0)
+        new_mom_ref[component] = kick[at : at + per_device, :]
     for copy in sent:
         copy.wait_send()
 
@@ -431,19 +453,24 @@
     slots = neighbours.shape[0]
     ghosts = ghost_rows.shape[0] // 2
     devices = lax.axis_size("bead")
-    consts = tables(devices, per_device)
-    rows = consts[0].shape[1]
+    table = tables(devices, per_device)
+    rows = -(-6 * per_device // TILE) * TILE
     cover = max(atoms // (devices // CB), LANES)
     vmem = pl.BlockSpec(memory_space=pltpu.VMEM)
-    smem = pl.BlockSpec(memory_space=pltpu.SMEM)
+    hbm = pl.BlockSpec(memory_space=pltpu.HBM)
     f32 = jnp.float32
     dma = pltpu.SemaphoreType.DMA
-    shape = jax.ShapeDtypeStruct(positions.shape, f32)
-    return pl.pallas_call(
+    operands = (
+        positions.transpose(1, 0, 2), momenta.transpose(1, 0, 2), neighbours,
+        ghost_rows.reshape(2, ghosts), species.reshape(1, atoms), species_scale.reshape(1, -1),
+        mass_table.reshape(1, -1), w_in.T, w_out, table,
+    )
+    shape = jax.ShapeDtypeStruct(operands[0].shape, f32)
+    new_positions, new_momenta = pl.pallas_call(
         cycle_kernel,
         name="cycle",
         out_shape=(shape, shape),
-        in_specs=[vmem] * 5 + [smem] * 2 + [vmem] * 7,
+        in_specs=[hbm] * 10,
         out_specs=(vmem, vmem),
         scratch_shapes=[
             pltpu.VMEM((NINNER + 1, rows, atoms), f32),
@@ -458,6 +485,9 @@
             pltpu.VMEM((2, TILE, ghosts), f32),
             pltpu.VMEM((2, TILE, ghosts), f32),
             pltpu.VMEM((2, devices, TILE, cover), f32),
+            *[pltpu.VMEM(operand.shape, operand.dtype) for operand in operands[:-1]],
+            pltpu.VMEM(table.shape[1:], f32),
+            dma((len(operands),)),
             dma((devices,)), dma((devices,)),
             dma((NINNER + 1, 2)), dma((NINNER + 1, 2)),
             dma((2,)), dma((2,)),
@@ -465,12 +495,10 @@
             dma((2, devices)), dma((2, devices)),
         ],
         compiler_params=pltpu.CompilerParams(
-            collective_id=0, has_side_effects=True, vmem_limit_bytes=32 * 1024 * 1024
+            collective_id=0, has_side_effects=True, vmem_limit_bytes=67043328
         ),
-    )(
-        positions, momenta, neighbours, ghost_rows.reshape(2, ghosts), species.reshape(1, atoms),
-        species_scale, mass_table, w_in, w_out, *consts,
-    )
+    )(*operands)
+    return (new_positions.transpose(1, 0, 2), new_momenta.transpose(1, 0, 2))
 
 
 def solution(mesh):

time: 60.6 us -> 55.3 us (0.913)
  local copies, waits for them, and re-layouts: 7.18 us -> 1.96 us
    unnamed x25 -> x4, local copies, waits for them, and re-layouts: 5.94 us -> 1.96 us
    pallas_call x2 -> x0, local copies, waits for them, and re-layouts: 1.24 us -> none  [body(): pl.pallas_call(cycle_kernel, name='cycle', out_shape=(shape, shape), in_s...]
where the time goes in v2:
time: 55.3 us; the launch traced here: 55.1 us
  Pallas kernels  52.5 us (95%)
  local copies, waits for them, and re-layouts  1.96 us (4%)
  between operations  0.65 us (1%)
    pallas_call x1, Pallas kernels, body(): pl.pallas_call(cycle_kernel, name='cycle', out_shape=(shape, shape), in_s...  52.5 us
    unnamed x4, local copies, waits for them, and re-layouts  1.96 us

profile of v2, /device:TPU:0, one launch (start us, length us, event | category | flops | bytes accessed | tf_op | source)
XLA Modules:
  0.0 55.1 jit_solution(10438184658909450955)
XLA Ops:
  0.6 52.5 %cycle.1 = (f32[3,4,512]{2,1,0:T(4,128)}, f32[3,4,512]{2,1,0:T(4,128)}) custom-call(f32[3,4,512]{2,1,0:T(4,128)} %bitcast.9, f32[3,4,512]{2,1,0:T(4,128)} %bitcast.10, s32[32,512]{1,0:T(8,128)} %near_in.1, s32[2,128]{1,0:T(2,128)} %bitcast.15, s32[1,512]{1,0:T(1,128)} %bitcast.14, f32[1,2]{1,0:T(1,128)} %bitcast.16, f32[1,2]{1,0:T(1,128)} %bitcast.17, ...), custom_call_target="tpu_custom_call" | custom-call | tf_op jit(solution)/shard_map/cycle/pallas_call | solution.py:469
  53.1 0.0 copy-start
  53.1 1.4 %copy.14 = f32[4,3,512]{2,0,1:T(4,128)} copy(f32[4,3,512]{2,0,1:T(4,128)} %bitcast.12) | data formatting | bytes 49152
  54.5 0.0 copy-done
  54.5 0.6 %copy.15 = f32[4,3,512]{2,0,1:T(4,128)} copy(f32[4,3,512]{2,0,1:T(4,128)S(1)} %bitcast.11) | data formatting | bytes 49152
Async XLA Ops:
  53.1 1.4 %copy-start = (f32[3,4,512]{2,1,0:T(4,128)S(1)}, f32[3,4,512]{2,1,0:T(4,128)}, u32[]{:S(2)}) copy-start(f32[3,4,512]{2,1,0:T(4,128)} %get-tuple-element.5) | copy-start | bytes 73732

commit v3 on v2

--- a/solution.py
+++ b/solution.py
@@ -114,9 +114,9 @@
     pos_in, mom_in, near_in, ghost_from, species_in, scale_in, mass_in, w_in_in, w_out_in, table_in,
     new_pos_ref, new_mom_ref,
     state, kick, weight, gathered, ghost_out, ghost_in, part_out, part_in, whole,
-    qghost_out, qghost_in, piece,
+    qghost_out, qghost_in, piece, edge_out, edge_in,
     pos_ref, mom_ref, near_ref, ghost_ref, species_ref, scale_ref, mass_ref, w_in_ref, w_out_ref,
-    table_ref, load_s,
+    table_ref, load_s, edge_s, edge_r,
     part_s, part_r, ghost_s, ghost_r, qghost_s, qghost_r, all_s, all_r, piece_s, piece_r,
 ):
     _, per_device, atoms = pos_ref.shape
@@ -154,7 +154,10 @@
     for j in range(1, devices):
         pl.semaphore_signal(barrier, inc=1, device_id={"bead": peers[j]}, device_id_type=MESH)
     for target in (above, below):
-        pl.semaphore_signal(barrier, inc=1, device_id={"space": target}, device_id_type=MESH)
+        for j in range(devices):
+            pl.semaphore_signal(
+                barrier, inc=1, device_id={"bead": peers[j], "space": target}, device_id_type=MESH
+            )
 
     def to_peer(src, dst, send, recv, j):
         return pltpu.make_async_remote_copy(
@@ -167,6 +170,23 @@
             src_ref=src, dst_ref=dst, send_sem=send.at[side], recv_sem=recv.at[side],
             device_id={"space": (above, below)[side]}, device_id_type=MESH,
         )
+
+    def to_edge(step, side, j):
+        return pltpu.make_async_remote_copy(
+            src_ref=edge_out.at[step, side], dst_ref=edge_in.at[step, side, me],
+            send_sem=edge_s.at[step, side, j], recv_sem=edge_r.at[step, side, j],
+            device_id={"bead": peers[j], "space": (above, below)[side]}, device_id_type=MESH,
+        )
+
+    def await_edges(step):
+        for side in range(2):
+            for j in range(devices):
+                pltpu.make_async_remote_copy(
+                    src_ref=edge_out.at[step, side], dst_ref=edge_in.at[step, side, senders[j]],
+                    send_sem=edge_s.at[step, side, j], recv_sem=edge_r.at[step, side, j],
+                    device_id={"bead": peers[j], "space": (above, below)[side]},
+                    device_id_type=MESH,
+                ).wait_recv()
 
     def row_of(component, kind, bead):
         return (component * 2 + kind) * per_device + bead
@@ -359,7 +379,7 @@
     ghost_copies = send_ghosts(0, jnp.broadcast_to(charge, (TILE, atoms)))
     whole[1] = jnp.broadcast_to(charge * inverse, (TILE, atoms))
 
-    pl.semaphore_wait(barrier, devices + 1)
+    pl.semaphore_wait(barrier, 3 * devices - 1)
     start(copies)
     start(ghost_copies)
     await_blocks(part_in, part_s, part_r)
@@ -416,10 +436,16 @@
             extra = both[moved_row:]
             whole[0] = extra
         state[step] = fresh
-        ghost_copies = send_ghosts(step, extra)
-        start(ghost_copies)
-        for copy in ghost_copies:
-            copy.wait_recv()
+        if step == 1:
+            ghost_copies = send_ghosts(step, extra)
+            start(ghost_copies)
+            for copy in ghost_copies:
+                copy.wait_recv()
+        else:
+            await_edges(step - 2)
+            for side in range(2):
+                edge = edge_in[step - 2, side].reshape(full, ghosts)
+                ghost_in[step, side] = dot(table_ref[0 : moved_row + TILE, 0:full], edge)
         if step == NINNER:
             learned(lambda c: ghost_window(ghost_in, (step,), rows + c), 1)
             start(send_piece(1))
@@ -431,6 +457,12 @@
                         all_s.at[step], all_r.at[step], j)
                 for j in range(1, devices)
             ])
+            for side in range(2):
+                for at in range(0, rows, TILE):
+                    block = gathered[step, me, at : at + TILE, :]
+                    for g, part in enumerate(ghost_rows_of(block, side)):
+                        edge_out[step - 1, side, at : at + TILE, g * LANES : (g + 1) * LANES] = part
+                start([to_edge(step - 1, side, j) for j in range(devices)])
             await_blocks(gathered.at[step], all_s.at[step], all_r.at[step])
 
     await_blocks(piece.at[1], piece_s.at[1], piece_r.at[1])
@@ -485,9 +517,12 @@
             pltpu.VMEM((2, TILE, ghosts), f32),
             pltpu.VMEM((2, TILE, ghosts), f32),
             pltpu.VMEM((2, devices, TILE, cover), f32),
+            pltpu.VMEM((NINNER - 1, 2, rows, ghosts), f32),
+            pltpu.VMEM((NINNER - 1, 2, devices, rows, ghosts), f32),
             *[pltpu.VMEM(operand.shape, operand.dtype) for operand in operands[:-1]],
             pltpu.VMEM(table.shape[1:], f32),
             dma((len(operands),)),
+            dma((NINNER - 1, 2, devices)), dma((NINNER - 1, 2, devices)),
             dma((devices,)), dma((devices,)),
             dma((NINNER + 1, 2)), dma((NINNER + 1, 2)),
             dma((2,)), dma((2,)),

time: 55.3 us -> 54.5 us (0.986)
  Pallas kernels: 52.5 us -> 51.6 us
    pallas_call x1, Pallas kernels: 52.5 us -> 51.6 us  [body(): pl.pallas_call(cycle_kernel, name='cycle', out_shape=(shape, shape), in_s...]
where the time goes in v3:
time: 54.5 us; the launch traced here: 54.3 us
  Pallas kernels  51.6 us (95%)
  local copies, waits for them, and re-layouts  1.96 us (4%)
  between operations  0.65 us (1%)
    pallas_call x1, Pallas kernels, body(): pl.pallas_call(cycle_kernel, name='cycle', out_shape=(shape, shape), in_s...  51.6 us
    unnamed x4, local copies, waits for them, and re-layouts  1.96 us

profile of v3, /device:TPU:0, one launch (start us, length us, event | category | flops | bytes accessed | tf_op | source)
XLA Modules:
  0.0 54.3 jit_solution(6794491219438597272)
XLA Ops:
  0.6 51.6 %cycle.1 = (f32[3,4,512]{2,1,0:T(4,128)}, f32[3,4,512]{2,1,0:T(4,128)}) custom-call(f32[3,4,512]{2,1,0:T(4,128)} %bitcast.9, f32[3,4,512]{2,1,0:T(4,128)} %bitcast.10, s32[32,512]{1,0:T(8,128)} %near_in.1, s32[2,128]{1,0:T(2,128)} %bitcast.15, s32[1,512]{1,0:T(1,128)} %bitcast.14, f32[1,2]{1,0:T(1,128)} %bitcast.16, f32[1,2]{1,0:T(1,128)} %bitcast.17, ...), custom_call_target="tpu_custom_call" | custom-call | tf_op jit(solution)/shard_map/cycle/pallas_call | solution.py:501
  52.3 0.0 copy-start
  52.3 1.4 %copy.14 = f32[4,3,512]{2,0,1:T(4,128)} copy(f32[4,3,512]{2,0,1:T(4,128)} %bitcast.12) | data formatting | bytes 49152
  53.7 0.0 copy-done
  53.7 0.6 %copy.15 = f32[4,3,512]{2,0,1:T(4,128)} copy(f32[4,3,512]{2,0,1:T(4,128)S(1)} %bitcast.11) | data formatting | bytes 49152
Async XLA Ops:
  52.3 1.4 %copy-start = (f32[3,4,512]{2,1,0:T(4,128)S(1)}, f32[3,4,512]{2,1,0:T(4,128)}, u32[]{:S(2)}) copy-start(f32[3,4,512]{2,1,0:T(4,128)} %get-tuple-element.5) | copy-start | bytes 73732
